TPU v7x, 256 devices: a whole 4x4x8 slice. The times are simulated.
256 devices in a mesh: group: 8 (over x, core), member: 32 (over y, z).
Axes of the slice: x: 4, y: 4, z: 8, core: 2. Of those that a mesh axis runs over, the one named last changes fastest.
Arguments:
- q_rows: bfloat16 [65536, 8192], P(('group', 'member')), may hold values from -36 to 36
- own_kv: bfloat16 [65536, 1024], P(('group', 'member')), may hold values from -6 to 6
- cache: bfloat16 [1024, 64, 1024], P(('group', 'member')), may hold values from -6 to 6
- recomp_hidden: bfloat16 [512, 8, 16, 4096], P(('group', 'member')), may hold values from -6 to 6
- w_kv: bfloat16 [4096, 1024], P('member', 'group'), may hold values from -0.09375 to 0.09375
- retrieval: int32 [512, 8], P(('group', 'member')), may hold values from 0 to 127, as said below
- positions: int32 [512, 8, 16], P(('group', 'member')), may hold values from 0 to 63, as said below
Outputs:
- attn_out: bfloat16 [65536, 8192], P(('group', 'member'))
Inputs may be any that keep to these rules, and one draw needn't show every extreme that they name: `retrieval`: the 8 passages of one query are different. Passage i of a group's corpus is held by the device of member index i // 4 in that group. The queries of one device name at most 1 passages held by any one device, and this bound is reached. The 16 positions of one retrieved passage are different.
All inputs are finite; a program needn't handle non-finite values.
Results may differ from a plain program's by a relative error of at most 0.0054.
Values may be sent and summed in bfloat16 or wider, within the bound.
A program may use at most 128 MiB of HBM per device.

v0:
```python
import jax
import jax.numpy as jnp
from jax import lax
from jax.sharding import PartitionSpec as P

D = 4096
HQ = 64
KVH = 4
HD = 128
TOPP = 8
QLEN = 128
PLEN = 64
RECOMP = 16
EPSILON = 1e-06


def local(q_rows, own_kv, cache, recomp_hidden, w_kv, retrieval, positions):
    query_count = retrieval.shape[0]
    requests = query_count * TOPP
    kv_width = 2 * KVH * HD
    grouped = HQ // KVH
    span_keys = TOPP * PLEN + QLEN
    scale = 1.0 / HD**0.5
    row_count = requests * RECOMP
    hidden = recomp_hidden.reshape(row_count, D).astype(jnp.float32)
    normed = (
        hidden * lax.rsqrt(jnp.mean(hidden * hidden, axis=1, keepdims=True) + EPSILON)
    ).astype(jnp.bfloat16)
    head_columns = lax.all_gather(w_kv, "group", axis=1, tiled=True)
    projected = jnp.dot(
        normed,
        lax.all_gather(head_columns, "member", axis=0, tiled=True),
        preferred_element_type=jnp.float32,
    )
    recomputed = projected.astype(jnp.bfloat16).reshape(requests, RECOMP, kv_width)
    wanted = retrieval.reshape(requests)
    pass_local = cache.shape[0]
    holders_count = lax.axis_size("member")
    my_index = lax.axis_index("member")
    capacity = -(-requests // holders_count)
    request_table = lax.all_gather(wanted.reshape(1, requests), "member", axis=0, tiled=True)
    mine_mask = request_table // pass_local == my_index
    earlier_mask = (jnp.arange(requests)[:, None] < jnp.arange(requests)[None, :]).astype(jnp.int32)
    slot_rank = jnp.dot(mine_mask.astype(jnp.int32), earlier_mask)
    slot_table = mine_mask[:, None, :] & (
        slot_rank[:, None, :] == jnp.arange(capacity)[None, :, None]
    )
    local_index = jnp.sum(
        jnp.where(slot_table, (request_table % pass_local)[:, None, :], 0), axis=2
    )
    slot_filled = jnp.any(slot_table, axis=2)
    outgoing = jnp.where(
        slot_filled[:, :, None, None], cache[local_index], jnp.zeros((), cache.dtype)
    )
    arrived = lax.all_to_all(outgoing, "member", split_axis=0, concat_axis=0, tiled=True)
    holder_of = wanted // pass_local
    same_holder = holder_of[:, None] == holder_of[None, :]
    before_me = jnp.arange(requests)[None, :] < jnp.arange(requests)[:, None]
    copy_rank = jnp.sum((same_holder & before_me).astype(jnp.int32), axis=1)
    blocks = arrived.reshape(holders_count * capacity, PLEN, kv_width)[
        holder_of * capacity + copy_rank
    ]
    spots = positions.reshape(requests, RECOMP)
    onehot = spots[:, :, None] == jnp.arange(PLEN)[None, None, :]
    covered = jnp.any(onehot, axis=1)
    placed = jnp.einsum(
        "krp,kre->kpe", onehot.astype(jnp.bfloat16), recomputed, preferred_element_type=jnp.float32
    ).astype(jnp.bfloat16)
    context = jnp.where(covered[:, :, None], placed, blocks).reshape(
        query_count, TOPP * PLEN, kv_width
    )
    context = jnp.concatenate([context, own_kv.reshape(query_count, QLEN, kv_width)], axis=1)
    keys = context[:, :, : KVH * HD].reshape(query_count, span_keys, KVH, HD)
    values = context[:, :, KVH * HD :].reshape(query_count, span_keys, KVH, HD)
    queries = q_rows.reshape(query_count, QLEN, KVH, grouped, HD)
    token_pos = jnp.arange(QLEN)[:, None]
    key_pos = jnp.arange(span_keys)[None, :]
    visible = (key_pos < TOPP * PLEN) | (key_pos - TOPP * PLEN <= token_pos)

    def attend(operands):
        query_block, key_block, value_block = operands
        scores = (
            jnp.einsum("tkgd,skd->kgts", query_block, key_block, preferred_element_type=jnp.float32)
            * scale
        )
        scores = jnp.where(visible, scores, -jnp.inf)
        peak = jnp.max(scores, axis=-1, keepdims=True)
        expd = jnp.exp(scores - peak)
        probs = (expd / jnp.sum(expd, axis=-1, keepdims=True)).astype(jnp.bfloat16)
        output = jnp.einsum(
            "kgts,skd->tkgd", probs, value_block, preferred_element_type=jnp.float32
        )
        return output.astype(jnp.bfloat16).reshape(QLEN, HQ * HD)

    results = lax.map(attend, (queries, keys, values))
    return results.reshape(query_count * QLEN, HQ * HD)


def solution(mesh):
    placed = (
        P(("group", "member"), None),
        P(("group", "member"), None),
        P(("group", "member"), None, None),
        P(("group", "member"), None, None, None),
        P("member", "group"),
        P(("group", "member"), None),
        P(("group", "member"), None, None),
    )
    return jax.shard_map(
        local, mesh=mesh, in_specs=placed, out_specs=P(("group", "member"), None), check_vma=False
    )
```

profile of v0, /device:TPU:32, one launch (start us, length us, event | category | flops | bytes accessed | tf_op | source)
XLA Modules:
  0.0 287.2 jit_solution(2852515802772880683)
XLA Ops:
  6.5 13.6 %all_gather.9 = bf16[128,1024]{1,0:T(8,128)(2,1)} all-gather(bf16[128,128]{1,0:T(8,128)(2,1)} %param.13), channel_id=1, replica_groups=mesh['group'=8,'member'=32] {'group'}, dimensions={1}, use_global_device_ids=true | all-gather | bytes 294912 | tf_op jit(solution)/shard_map/all_gather | solution.py:29
  21.0 40.2 %all-gather = s32[32,1,16]{2,1,0:T(1,128)S(1)} all-gather(s32[1,1,16]{2,1,0:T(1,128)S(1)} %reshape.252), channel_id=1, replica_groups=mesh['group'=8,'member'=32] {'member'}, dimensions={0}, use_global_device_ids=true | all-gather | bytes 2112 | tf_op jit(solution)/shard_map/all_gather | solution.py:41
  61.5 2.8 gather_fusion
  64.4 4.5 %bitcast_select_fusion.4 = bf16[32,1,64,1024]{3,2,1,0:T(8,128)(2,1)} fusion(bf16[32,64,1024]{2,1,0:T(8,128)(2,1)} %gather_fusion, pred[32]{0:T(512)(128)(4,1)S(1)} %reduce_or.19), kind=kLoop, calls=%fused_computation.31 | loop fusion | flops 2097152 | bytes 8388640 | tf_op jit(solution)/shard_map/jit(_where)/select_n | solution.py:52
  68.9 8.1 %all-to-all-start = ((bf16[32,1,64,1024]{3,2,1,0:T(8,128)(2,1)}), bf16[32,1,64,1024]{3,2,1,0:T(8,128)(2,1)}, u32[]{:S(2)}, u32[]{:S(2)}) async-start(bf16[32,1,64,1024]{3,2,1,0:T(8,128)(2,1)} %bitcast_select_fusion.4), calls=%async_computation | async-start | bytes 8388608 | tf_op jit(solution)/shard_map/all_to_all | solution.py:55
  78.1 5.4 %copy.46 = bf16[32,8,64,128]{3,2,1,0:T(8,128)(2,1)} copy(bf16[32,8,64,128]{3,1,2,0:T(8,128)(2,1)} %bitcast.134) | data formatting | bytes 8388608
  83.8 1.9 fusion.30
  85.7 118.0 %all-to-all-done = bf16[32,1,64,1024]{3,2,1,0:T(8,128)(2,1)} async-done(((bf16[32,1,64,1024]{3,2,1,0:T(8,128)(2,1)}), bf16[32,1,64,1024]{3,2,1,0:T(8,128)(2,1)}, u32[]{:S(2)}, u32[]{:S(2)}) %all-to-all-start) | async-done | bytes 4194336 | tf_op jit(solution)/shard_map/all_to_all | solution.py:55
  203.7 2.9 gather_fusion.1
  206.6 6.3 %convolution_convert_fusion = bf16[256,1024]{1,0:T(8,128)(2,1)S(1)} fusion(bf16[256,4096]{1,0:T(8,128)(2,1)} %fusion.30, bf16[4096,1024]{1,0:T(8,128)(2,1)} %all-gather.3.cloned.1.call-done), kind=kOutput, calls=%fused_computation.40 | convolution fusion | flops 2147745792 | bytes 11010048 | tf_op jit(solution)/shard_map/dot_general | solution.py:30
  213.0 2.6 convert_select_fusion
  215.6 2.9 copy.34
  218.4 1.7 pad_maximum_fusion
  220.2 59.2 %while.11 = (s32[]{:T(128)}, bf16[2,128,8192]{2,1,0:T(8,128)(2,1)}, bf16[2,640,4,128]{1,3,2,0:T(8,128)(2,1)}, bf16[2,640,4,128]{1,3,2,0:T(8,128)(2,1)}, bf16[2,1...) while((s32[]{:T(128)}, bf16[2,128,8192]{2,1,0:T(8,128)(2,1)}, ...), condition=%wide.region_8.9_spmd.clone, body=%wide.region_5.8_spmd.clone.sunk | while | flops 2717024768 | bytes 60265176 | solution.py:95
  220.2 2.0 constant_dynamic-slice_fusion.2
  222.4 12.5 %fusion.73 = (f32[4,16,128]{2,1,0:T(8,128)S(1)}, f32[4,16,128,640]{2,3,1,0:T(8,128)}) fusion(pred[128,640]{0,1:T(8,128)(4,1)S(1)} %fusion.72, bf16[1,128,4,16,128]{4,3,2,1,0:T(8,128)(2,1)S(1)} %constant_dynamic-slice_fusion.2, bf16[2,640,4,128]{1,3,2,0:T(8,128)(2,1)} %get-tuple-element.170, s32[]{:T(128)} %get-tuple-element.159), kind=kOutput, calls=%fused_computation.92.clone.1 | convolution fusion | flops 1363149440 | bytes 23839232 | tf_op jit(solution)/shard_map/while/body/eval_jaxpr/sub | solution.py:88
  234.9 10.4 %fusion.74 = bf16[4,128,16,128]{3,1,2,0:T(8,128)(2,1)} fusion(f32[4,16,128,640]{2,3,1,0:T(8,128)} %get-tuple-element.149, f32[4,16,128]{2,1,0:T(8,128)S(1)} %get-tuple-element.150, bf16[2,640,4,128]{1,3,2,0:T(8,128)(2,1)} %get-tuple-element.169, s32[]{:T(128)} %get-tuple-element.159), kind=kOutput, calls=%fused_computation.14.clone.1 | convolution fusion | flops 1353711616 | bytes 23757312 | tf_op jit(solution)/shard_map/while/body/eval_jaxpr/kgts,skd->tkgd/dot_general | solution.py:90
  245.4 2.9 %copy.61 = bf16[1,128,8192]{2,1,0:T(8,128)(2,1)S(1)} copy(bf16[1,128,8192]{1,2,0:T(8,128)(2,1)} %bitcast.131) | data formatting | bytes 4194304 | tf_op jit(solution)/shard_map/while/body/jit(dynamic_update_index_in_dim)/dynamic_update_slice | solution.py:95
  248.3 1.5 constant_dynamic-update-slice_fusion.2
  249.8 2.0 constant_dynamic-slice_fusion.2
  252.0 12.5 %fusion.73 = (f32[4,16,128]{2,1,0:T(8,128)S(1)}, f32[4,16,128,640]{2,3,1,0:T(8,128)}) fusion(pred[128,640]{0,1:T(8,128)(4,1)S(1)} %fusion.72, bf16[1,128,4,16,128]{4,3,2,1,0:T(8,128)(2,1)S(1)} %constant_dynamic-slice_fusion.2, bf16[2,640,4,128]{1,3,2,0:T(8,128)(2,1)} %get-tuple-element.170, s32[]{:T(128)} %get-tuple-element.159), kind=kOutput, calls=%fused_computation.92.clone.1 | convolution fusion | flops 1363149440 | bytes 23839232 | tf_op jit(solution)/shard_map/while/body/eval_jaxpr/sub | solution.py:88
  264.5 10.4 %fusion.74 = bf16[4,128,16,128]{3,1,2,0:T(8,128)(2,1)} fusion(f32[4,16,128,640]{2,3,1,0:T(8,128)} %get-tuple-element.149, f32[4,16,128]{2,1,0:T(8,128)S(1)} %get-tuple-element.150, bf16[2,640,4,128]{1,3,2,0:T(8,128)(2,1)} %get-tuple-element.169, s32[]{:T(128)} %get-tuple-element.159), kind=kOutput, calls=%fused_computation.14.clone.1 | convolution fusion | flops 1353711616 | bytes 23757312 | tf_op jit(solution)/shard_map/while/body/eval_jaxpr/kgts,skd->tkgd/dot_general | solution.py:90
  275.0 2.9 %copy.61 = bf16[1,128,8192]{2,1,0:T(8,128)(2,1)S(1)} copy(bf16[1,128,8192]{1,2,0:T(8,128)(2,1)} %bitcast.131) | data formatting | bytes 4194304 | tf_op jit(solution)/shard_map/while/body/jit(dynamic_update_index_in_dim)/dynamic_update_slice | solution.py:95
  277.9 1.5 constant_dynamic-update-slice_fusion.2
  (37 shorter events, 4.0 us)
Async XLA Ops:
  6.5 55.0 %copy-start = (bf16[4,64,1024]{2,1,0:T(8,128)(2,1)S(1)}, bf16[4,64,1024]{2,1,0:T(8,128)(2,1)}, u32[]{:S(2)}) copy-start(bf16[4,64,1024]{2,1,0:T(8,128)(2,1)} %param.11) | copy-start | bytes 1572868
  6.5 200.1 %all-gather.3.cloned.1.call-start = ((), (), s32[]{:S(2)}) async-start(), calls=%async_computation.1 | async-start | bytes 8650752 | tf_op jit(solution)/shard_map/all_gather | solution.py:32
  68.9 8.1 %copy-start.5 = (s32[2,8]{1,0:T(2,128)S(1)}, s32[2,8]{1,0:T(2,128)}, u32[]{:S(2)}) copy-start(s32[2,8]{1,0:T(2,128)} %param.14) | copy-start | bytes 196
  68.9 8.3 %copy-start.2 = (bf16[2,8,16,4096]{3,2,1,0:T(8,128)(2,1)S(1)}, bf16[2,8,16,4096]{3,2,1,0:T(8,128)(2,1)}, u32[]{:S(2)}) copy-start(bf16[2,8,16,4096]{3,2,1,0:T(8,128)(2,1)} %param.12) | copy-start | bytes 6291460
  68.9 8.9 %copy-start.3 = (bf16[256,1024]{1,0:T(8,128)(2,1)S(1)}, bf16[256,1024]{1,0:T(8,128)(2,1)}, u32[]{:S(2)}) copy-start(bf16[256,1024]{1,0:T(8,128)(2,1)} %param.10) | copy-start | bytes 1572868
  68.9 134.8 %all-to-all-start = ((bf16[32,1,64,1024]{3,2,1,0:T(8,128)(2,1)}), bf16[32,1,64,1024]{3,2,1,0:T(8,128)(2,1)}, u32[]{:S(2)}, u32[]{:S(2)}) async-start(bf16[32,1,64,1024]{3,2,1,0:T(8,128)(2,1)} %bitcast_select_fusion.4), calls=%async_computation | async-start | bytes 8388608 | tf_op jit(solution)/shard_map/all_to_all | solution.py:55
  78.0 5.6 %copy-start.4 = (s32[2,8,16]{2,1,0:T(8,128)S(1)}, s32[2,8,16]{2,1,0:T(8,128)}, u32[]{:S(2)}) copy-start(s32[2,8,16]{2,1,0:T(8,128)} %param.15) | copy-start | bytes 3076
  279.4 1.0 copy-start.1
Sparse Core Ops, SparseCore 0:
  20.3 181.5 all-gather.2
where the time goes:
time: 288 us; the launch traced here: 287 us
  waiting for transfers between devices  118 us (41%)
  matrix products  55.1 us (19%)
  blocking collectives  53.9 us (19%)
  local copies, waits for them, and re-layouts  29.1 us (10%)
  between operations  13.5 us (5%)
  other arithmetic  9.49 us (3%)
  starting transfers between devices  8.12 us (3%)
    all_to_all x1, waiting for transfers between devices, local(): lax.all_to_all(outgoing, 'member', split_axis=0, concat_axis=0, tiled=True)  118 us
    all_gather x1, blocking collectives, local(): lax.all_gather(wanted.reshape(1, requests), 'member', axis=0, tiled=True)  40.2 us
    sub x2, matrix products, attend(): expd = jnp.exp(scores - peak)  25.1 us
    dot_general x2, matrix products, attend(): jnp.einsum('kgts,skd->tkgd', probs, value_block, preferred_element_type=j...  20.9 us
    all_gather x1, blocking collectives, local(): head_columns = lax.all_gather(w_kv, 'group', axis=1, tiled=True)  13.6 us
    dynamic_update_slice x4, local copies, waits for them, and re-layouts, local(): results = lax.map(attend, (queries, keys, values))  8.71 us
    all_to_all x1, starting transfers between devices, local(): lax.all_to_all(outgoing, 'member', split_axis=0, concat_axis=0, tiled=True)  8.12 us
    unnamed x14, local copies, waits for them, and re-layouts  7.19 us
  transfers between devices with their start and end apart: 2, of which 1 were waited for; matrix products, arithmetic and copies ran while one was open for 7% of the time, Pallas kernels for 0%

commit v1 on v0

--- a/solution.py
+++ b/solution.py
@@ -38,7 +38,10 @@
     holders_count = lax.axis_size("member")
     my_index = lax.axis_index("member")
     capacity = -(-requests // holders_count)
-    request_table = lax.all_gather(wanted.reshape(1, requests), "member", axis=0, tiled=True)
+    load = wanted.reshape(1, requests)
+    base_arr = jnp.stack([load for _ in range(jax.lax.axis_size("member"))], axis=0)
+    top = jax.lax.all_to_all(base_arr, "member", 0, 0)
+    request_table = jnp.concatenate(top, axis=0)
     mine_mask = request_table // pass_local == my_index
     earlier_mask = (jnp.arange(requests)[:, None] < jnp.arange(requests)[None, :]).astype(jnp.int32)
     slot_rank = jnp.dot(mine_mask.astype(jnp.int32), earlier_mask)

time: 288 us -> 272 us (0.944)
  blocking collectives: 53.9 us -> 13.6 us
  waiting for transfers between devices: 118 us -> 131 us
  starting transfers between devices: 8.12 us -> 17.5 us
    all_gather x1 -> x0, blocking collectives: 40.2 us -> none  [local(): lax.all_gather(wanted.reshape(1, requests), 'member', axis=0, tiled=True)]
    all_to_all x0 -> x1, starting transfers between devices: none -> 11.4 us  [local(): top = jax.lax.all_to_all(base_arr, 'member', 0, 0)]
    all_to_all x0 -> x1, waiting for transfers between devices: none -> 8.6 us  [local(): top = jax.lax.all_to_all(base_arr, 'member', 0, 0)]
    all_to_all x1, waiting for transfers between devices: 118 us -> 123 us  [local(): lax.all_to_all(outgoing, 'member', split_axis=0, concat_axis=0, tiled=True)]
    unnamed x14 -> x13, local copies, waits for them, and re-layouts: 7.19 us -> 6.43 us
  transfers between devices with their start and end apart: 2 -> 3, of which waited for: 1 -> 2; matrix products, arithmetic and copies ran while one was open for 7% -> 8% of each run, Pallas kernels for 0% -> 0%
where the time goes in v1:
time: 272 us; the launch traced here: 270 us
  waiting for transfers between devices  131 us (48%)
  matrix products  55.1 us (20%)
  local copies, waits for them, and re-layouts  29.6 us (11%)
  starting transfers between devices  17.5 us (6%)
  blocking collectives  13.6 us (5%)
  between operations  13.5 us (5%)
  other arithmetic  9.49 us (3%)
    all_to_all x1, waiting for transfers between devices, local(): lax.all_to_all(outgoing, 'member', split_axis=0, concat_axis=0, tiled=True)  123 us
    sub x2, matrix products, attend(): expd = jnp.exp(scores - peak)  25.1 us
    dot_general x2, matrix products, attend(): jnp.einsum('kgts,skd->tkgd', probs, value_block, preferred_element_type=j...  20.9 us
    all_gather x1, blocking collectives, local(): head_columns = lax.all_gather(w_kv, 'group', axis=1, tiled=True)  13.6 us
    all_to_all x1, starting transfers between devices, local(): top = jax.lax.all_to_all(base_arr, 'member', 0, 0)  11.4 us
    dynamic_update_slice x4, local copies, waits for them, and re-layouts, local(): results = lax.map(attend, (queries, keys, values))  8.71 us
    all_to_all x1, waiting for transfers between devices, local(): top = jax.lax.all_to_all(base_arr, 'member', 0, 0)  8.6 us
    unnamed x13, local copies, waits for them, and re-layouts  6.43 us
  transfers between devices with their start and end apart: 3, of which 2 were waited for; matrix products, arithmetic and copies ran while one was open for 8% of the time, Pallas kernels for 0%

profile of v1, /device:TPU:32, one launch (start us, length us, event | category | flops | bytes accessed | tf_op | source)
XLA Modules:
  0.0 270.3 jit_solution(10718499953830397325)
XLA Ops:
  6.5 13.6 %all_gather.6 = bf16[128,1024]{1,0:T(8,128)(2,1)} all-gather(bf16[128,128]{1,0:T(8,128)(2,1)} %param.13), channel_id=1, replica_groups=mesh['group'=8,'member'=32] {'group'}, dimensions={1}, use_global_device_ids=true | all-gather | bytes 294912 | tf_op jit(solution)/shard_map/all_gather | solution.py:29
  21.6 11.4 %all-to-all-start = ((s32[32,1,16]{2,1,0:T(1,128)}), s32[32,1,16]{2,1,0:T(1,128)S(1)}, u32[]{:S(2)}, u32[]{:S(2)}) async-start(s32[32,1,16]{2,1,0:T(1,128)} %stack.3), calls=%async_computation | async-start | bytes 32768 | tf_op jit(solution)/shard_map/all_to_all | solution.py:43
  33.0 8.6 %all-to-all-done = s32[32,1,16]{2,1,0:T(1,128)S(1)} async-done(((s32[32,1,16]{2,1,0:T(1,128)}), s32[32,1,16]{2,1,0:T(1,128)S(1)}, u32[]{:S(2)}, u32[]{:S(2)}) %all-to-all-start) | async-done | bytes 2080 | tf_op jit(solution)/shard_map/all_to_all | solution.py:43
  41.9 2.8 %gather_fusion = bf16[32,64,1024]{2,1,0:T(8,128)(2,1)} fusion(bf16[4,64,1024]{2,1,0:T(8,128)(2,1)S(1)} %copy-done, s32[1024]{0:T(1024)S(1)} %pad_clamp_fusion.1), kind=kCustom, calls=%fused_computation | custom fusion | bytes 8388736 | tf_op jit(solution)/shard_map/gather | solution.py:56
  44.7 4.5 %bitcast_select_fusion.4 = bf16[32,1,64,1024]{3,2,1,0:T(8,128)(2,1)} fusion(bf16[32,64,1024]{2,1,0:T(8,128)(2,1)} %gather_fusion, pred[32]{0:T(512)(128)(4,1)S(1)} %reduce_or.19), kind=kLoop, calls=%fused_computation.31 | loop fusion | flops 2097152 | bytes 8388640 | tf_op jit(solution)/shard_map/jit(_where)/select_n | solution.py:55
  49.2 6.1 %all-to-all-start.1 = ((bf16[32,1,64,1024]{3,2,1,0:T(8,128)(2,1)}), bf16[32,1,64,1024]{3,2,1,0:T(8,128)(2,1)}, u32[]{:S(2)}, u32[]{:S(2)}) async-start(bf16[32,1,64,1024]{3,2,1,0:T(8,128)(2,1)} %bitcast_select_fusion.4), calls=%async_computation.1 | async-start | bytes 8388608 | tf_op jit(solution)/shard_map/all_to_all | solution.py:58
  56.3 5.4 %copy.43 = bf16[32,8,64,128]{3,2,1,0:T(8,128)(2,1)} copy(bf16[32,8,64,128]{3,1,2,0:T(8,128)(2,1)} %bitcast.134) | data formatting | bytes 8388608
  62.0 1.9 fusion.30
  64.0 122.8 %all-to-all-done.1 = bf16[32,1,64,1024]{3,2,1,0:T(8,128)(2,1)} async-done(((bf16[32,1,64,1024]{3,2,1,0:T(8,128)(2,1)}), bf16[32,1,64,1024]{3,2,1,0:T(8,128)(2,1)}, u32[]{:S(2)}, u32[]{:S(2)}) %all-to-all-start.1) | async-done | bytes 4194336 | tf_op jit(solution)/shard_map/all_to_all | solution.py:58
  186.8 2.9 %gather_fusion.1 = bf16[16,64,1024]{2,1,0:T(8,128)(2,1)S(1)} fusion(bf16[32,64,1024]{2,1,0:T(8,128)(2,1)} %bitcast.7, s32[1024]{0:T(1024)S(1)} %pad_clamp_fusion), kind=kCustom, calls=%fused_computation.1 | custom fusion | bytes 4194368 | tf_op jit(solution)/shard_map/gather | solution.py:63
  189.7 6.3 %convolution_convert_fusion = bf16[256,1024]{1,0:T(8,128)(2,1)S(1)} fusion(bf16[256,4096]{1,0:T(8,128)(2,1)} %fusion.30, bf16[4096,1024]{1,0:T(8,128)(2,1)} %all-gather.2.cloned.1.call-done), kind=kOutput, calls=%fused_computation.40 | convolution fusion | flops 2147745792 | bytes 11010048 | tf_op jit(solution)/shard_map/dot_general | solution.py:30
  196.1 2.6 convert_select_fusion
  198.6 2.9 %copy.31 = bf16[2,512,1024]{1,2,0:T(8,128)(2,1)S(1)} copy(bf16[2,512,1024]{2,1,0:T(8,128)(2,1)} %bitcast.133) | data formatting | bytes 4194304 | tf_op jit(solution)/shard_map/reshape | solution.py:72
  201.5 1.7 pad_maximum_fusion
  203.2 59.2 %while.11 = (s32[]{:T(128)}, bf16[2,128,8192]{2,1,0:T(8,128)(2,1)}, bf16[2,640,4,128]{1,3,2,0:T(8,128)(2,1)}, bf16[2,640,4,128]{1,3,2,0:T(8,128)(2,1)}, bf16[2,1...) while((s32[]{:T(128)}, bf16[2,128,8192]{2,1,0:T(8,128)(2,1)}, ...), condition=%wide.region_8.9_spmd.clone, body=%wide.region_5.8_spmd.clone.sunk | while | flops 2717024768 | bytes 60265176 | solution.py:98
  203.2 2.0 constant_dynamic-slice_fusion.2
  205.5 12.5 %fusion.73 = (f32[4,16,128]{2,1,0:T(8,128)S(1)}, f32[4,16,128,640]{2,3,1,0:T(8,128)}) fusion(pred[128,640]{0,1:T(8,128)(4,1)S(1)} %fusion.72, bf16[1,128,4,16,128]{4,3,2,1,0:T(8,128)(2,1)S(1)} %constant_dynamic-slice_fusion.2, bf16[2,640,4,128]{1,3,2,0:T(8,128)(2,1)} %get-tuple-element.170, s32[]{:T(128)} %get-tuple-element.159), kind=kOutput, calls=%fused_computation.92.clone.1 | convolution fusion | flops 1363149440 | bytes 23839232 | tf_op jit(solution)/shard_map/while/body/eval_jaxpr/sub | solution.py:91
  218.0 10.4 %fusion.74 = bf16[4,128,16,128]{3,1,2,0:T(8,128)(2,1)} fusion(f32[4,16,128,640]{2,3,1,0:T(8,128)} %get-tuple-element.149, f32[4,16,128]{2,1,0:T(8,128)S(1)} %get-tuple-element.150, bf16[2,640,4,128]{1,3,2,0:T(8,128)(2,1)} %get-tuple-element.169, s32[]{:T(128)} %get-tuple-element.159), kind=kOutput, calls=%fused_computation.14.clone.1 | convolution fusion | flops 1353711616 | bytes 23757312 | tf_op jit(solution)/shard_map/while/body/eval_jaxpr/kgts,skd->tkgd/dot_general | solution.py:93
  228.5 2.9 %copy.58 = bf16[1,128,8192]{2,1,0:T(8,128)(2,1)S(1)} copy(bf16[1,128,8192]{1,2,0:T(8,128)(2,1)} %bitcast.131) | data formatting | bytes 4194304 | tf_op jit(solution)/shard_map/while/body/jit(dynamic_update_index_in_dim)/dynamic_update_slice | solution.py:98
  231.4 1.5 constant_dynamic-update-slice_fusion.2
  232.8 2.0 constant_dynamic-slice_fusion.2
  235.1 12.5 %fusion.73 = (f32[4,16,128]{2,1,0:T(8,128)S(1)}, f32[4,16,128,640]{2,3,1,0:T(8,128)}) fusion(pred[128,640]{0,1:T(8,128)(4,1)S(1)} %fusion.72, bf16[1,128,4,16,128]{4,3,2,1,0:T(8,128)(2,1)S(1)} %constant_dynamic-slice_fusion.2, bf16[2,640,4,128]{1,3,2,0:T(8,128)(2,1)} %get-tuple-element.170, s32[]{:T(128)} %get-tuple-element.159), kind=kOutput, calls=%fused_computation.92.clone.1 | convolution fusion | flops 1363149440 | bytes 23839232 | tf_op jit(solution)/shard_map/while/body/eval_jaxpr/sub | solution.py:91
  247.6 10.4 %fusion.74 = bf16[4,128,16,128]{3,1,2,0:T(8,128)(2,1)} fusion(f32[4,16,128,640]{2,3,1,0:T(8,128)} %get-tuple-element.149, f32[4,16,128]{2,1,0:T(8,128)S(1)} %get-tuple-element.150, bf16[2,640,4,128]{1,3,2,0:T(8,128)(2,1)} %get-tuple-element.169, s32[]{:T(128)} %get-tuple-element.159), kind=kOutput, calls=%fused_computation.14.clone.1 | convolution fusion | flops 1353711616 | bytes 23757312 | tf_op jit(solution)/shard_map/while/body/eval_jaxpr/kgts,skd->tkgd/dot_general | solution.py:93
  258.1 2.9 %copy.58 = bf16[1,128,8192]{2,1,0:T(8,128)(2,1)S(1)} copy(bf16[1,128,8192]{1,2,0:T(8,128)(2,1)} %bitcast.131) | data formatting | bytes 4194304 | tf_op jit(solution)/shard_map/while/body/jit(dynamic_update_index_in_dim)/dynamic_update_slice | solution.py:98
  (38 shorter events, 6.0 us)
Async XLA Ops:
  6.5 35.3 %copy-start = (bf16[4,64,1024]{2,1,0:T(8,128)(2,1)S(1)}, bf16[4,64,1024]{2,1,0:T(8,128)(2,1)}, u32[]{:S(2)}) copy-start(bf16[4,64,1024]{2,1,0:T(8,128)(2,1)} %param.11) | copy-start | bytes 1572868
  6.5 183.2 %all-gather.2.cloned.1.call-start = ((), (), s32[]{:S(2)}) async-start(), calls=%async_computation.2 | async-start | bytes 8650752 | tf_op jit(solution)/shard_map/all_gather | solution.py:32
  21.6 20.0 %all-to-all-start = ((s32[32,1,16]{2,1,0:T(1,128)}), s32[32,1,16]{2,1,0:T(1,128)S(1)}, u32[]{:S(2)}, u32[]{:S(2)}) async-start(s32[32,1,16]{2,1,0:T(1,128)} %stack.3), calls=%async_computation | async-start | bytes 32768 | tf_op jit(solution)/shard_map/all_to_all | solution.py:43
  49.2 6.1 %copy-start.5 = (s32[2,8]{1,0:T(2,128)S(1)}, s32[2,8]{1,0:T(2,128)}, u32[]{:S(2)}) copy-start(s32[2,8]{1,0:T(2,128)} %param.14) | copy-start | bytes 196
  49.2 6.2 %copy-start.2 = (bf16[2,8,16,4096]{3,2,1,0:T(8,128)(2,1)S(1)}, bf16[2,8,16,4096]{3,2,1,0:T(8,128)(2,1)}, u32[]{:S(2)}) copy-start(bf16[2,8,16,4096]{3,2,1,0:T(8,128)(2,1)} %param.12) | copy-start | bytes 6291460
  49.2 6.8 %copy-start.3 = (bf16[256,1024]{1,0:T(8,128)(2,1)S(1)}, bf16[256,1024]{1,0:T(8,128)(2,1)}, u32[]{:S(2)}) copy-start(bf16[256,1024]{1,0:T(8,128)(2,1)} %param.10) | copy-start | bytes 1572868
  49.2 137.6 %all-to-all-start.1 = ((bf16[32,1,64,1024]{3,2,1,0:T(8,128)(2,1)}), bf16[32,1,64,1024]{3,2,1,0:T(8,128)(2,1)}, u32[]{:S(2)}, u32[]{:S(2)}) async-start(bf16[32,1,64,1024]{3,2,1,0:T(8,128)(2,1)} %bitcast_select_fusion.4), calls=%async_computation.1 | async-start | bytes 8388608 | tf_op jit(solution)/shard_map/all_to_all | solution.py:58
  56.3 5.6 %copy-start.4 = (s32[2,8,16]{2,1,0:T(8,128)S(1)}, s32[2,8,16]{2,1,0:T(8,128)}, u32[]{:S(2)}) copy-start(s32[2,8,16]{2,1,0:T(8,128)} %param.15) | copy-start | bytes 3076
  262.4 1.0 copy-start.1
Sparse Core Ops, SparseCore 0:
  20.3 167.9 all-gather.1
